TPU v7x, 128 devices: a whole 4x4x4 slice. The times are simulated.
128 devices in a mesh: sec: 4 (over y), dp: 8 (over x_hi, z), mp: 4 (over x_lo, core).
Axes of the slice: x: 4 (x_hi: 2, x_lo: 2; x = x_hi * 2 + x_lo), y: 4, z: 4, core: 2. Of those that a mesh axis runs over, the one named last changes fastest.
Arguments:
- patches: bfloat16 [320, 5120], P('dp'), may hold values from -6 to 6
- ln_gain: bfloat16 [1280], replicated, may hold values from 0.099609375 to 1.8984375
- ln_shift: bfloat16 [1280], replicated, may hold values from -3 to 3
- w_in: bfloat16 [5120, 5120], P('dp', ('sec', 'mp')), may hold values from -0.078125 to 0.078125
- b_in: bfloat16 [5120], P(('sec', 'mp')), may hold values from -3 to 3
- w_out: bfloat16 [5120, 8192], P(('sec', 'mp'), 'dp'), may hold values from -0.125 to 0.125
- b_out: bfloat16 [8192], P(('sec', 'mp')), may hold values from -3 to 3
- place: int32 [320], P('dp'), may hold values from 0 to 255, as said below
- image_counts: int32 [8], P('dp'), may hold values from 1 to 40, 128 in all
- text_rows: bfloat16 [2048, 8192], P('dp', ('sec', 'mp')), may hold values from -6 to 6
- segments: int32 [8, 256], P('dp'), may hold values from 0 to 3, never falling along the last dimension, each value on 1 to 128 neighbouring positions
- norm_gain: bfloat16 [2, 8192], replicated, may hold values from 0.099609375 to 1.8984375
- q_weight: bfloat16 [2, 8192, 4096], P(None, None, ('sec', 'mp'))
- kv_weight: bfloat16 [2, 2, 512, 8192], P(None, None, ('sec', 'mp'))
- o_weight: bfloat16 [2, 4096, 8192], P(None, ('sec', 'mp')), may hold values from -0.125 to 0.125
- grad_rows: bfloat16 [320, 8192], P('dp'), may hold values from -6 to 6
Outputs:
- final_rows: float32 [2048, 8192], P('dp', ('sec', 'mp'))
- patch_grads: float32 [320, 5120], P('dp')
Inputs may be any that keep to these rules, and one draw needn't show every extreme that they name: `place`: each owner's 40 entries are distinct token positions of its own packed sequence; only an owner's first image_counts entries are used. `image_counts`: the counts sum to 8 * (16) over all owners.
All inputs are finite; a program needn't handle non-finite values. No bound on the sum of `image_counts` on one device may be relied on, other than what follows from the above.
Results may differ from a plain program's by a relative error of at most 0.0055.
Values may be sent and summed in bfloat16 or wider, within the bound.
A program may use at most 128 MiB of HBM per device.

v0:
```python
import math
import jax
import jax.numpy as jnp
from jax import lax
from jax.sharding import PartitionSpec as P

D = 8192
HEAD_DIM = 128
ln_eps = 1e-06
rms_eps = 1e-06
rope_base = 1000000.0


def group_norm(patch_rows, ln_gain, ln_shift):
    row_count = patch_rows.shape[0]
    grouped = patch_rows.astype(jnp.float32).reshape(row_count, -1, ln_gain.shape[0])
    center = grouped - jnp.mean(grouped, axis=-1, keepdims=True)
    spread = jnp.mean(center * center, axis=-1, keepdims=True)
    scaled = center * lax.rsqrt(spread + ln_eps) * ln_gain.astype(jnp.float32) + ln_shift.astype(
        jnp.float32
    )
    return scaled.reshape(row_count, -1)


def gelu_exact(values):
    return jax.nn.gelu(values, approximate=False)


def rotate(values, positions):
    head_depth = values.shape[-1]
    half_depth = head_depth // 2
    inv_freq = rope_base ** (-2.0 * jnp.arange(half_depth, dtype=jnp.float32) / head_depth)
    angles = positions[:, None] * inv_freq[None, :]
    cosine = jnp.cos(angles)[:, None, :]
    sine_part = jnp.sin(angles)[:, None, :]
    first_half = values[..., :half_depth]
    second = values[..., half_depth:]
    return jnp.concatenate(
        [first_half * cosine - second * sine_part, second * cosine + first_half * sine_part],
        axis=-1,
    )


def doc_mask(segment_ids):
    token_index = jnp.arange(segment_ids.shape[0], dtype=jnp.int32)
    same_doc = segment_ids[:, None] == segment_ids[None, :]
    allowed = same_doc & (token_index[None, :] <= token_index[:, None])
    positions = jnp.sum(allowed.astype(jnp.int32), axis=1) - 1
    return (allowed, positions.astype(jnp.float32))


def attend(normed, allowed, positions, q_local, kv_local):
    token_count = normed.shape[0]
    queries = jnp.dot(normed, q_local, preferred_element_type=jnp.float32).reshape(
        token_count, -1, HEAD_DIM
    )
    key_value = jnp.einsum("td,kcd->tkc", normed, kv_local, preferred_element_type=jnp.float32)
    key_value = lax.all_gather(key_value, "mp", axis=2, tiled=True)
    key_rows = rotate(key_value[:, 0:1, :], positions)[:, 0, :].astype(jnp.bfloat16)
    value_rows = key_value[:, 1, :].astype(jnp.bfloat16)
    queries = rotate(queries, positions).astype(jnp.bfloat16)
    scores = jnp.einsum("thd,sd->hts", queries, key_rows, preferred_element_type=jnp.float32) * (
        1.0 / math.sqrt(HEAD_DIM)
    )
    scores = jnp.where(allowed[None], scores, -jnp.inf)
    row_max = jnp.max(scores, axis=-1, keepdims=True)
    exp_scores = jnp.exp(scores - row_max)
    attn_weights = (exp_scores / jnp.sum(exp_scores, axis=-1, keepdims=True)).astype(jnp.bfloat16)
    attended = jnp.einsum(
        "hts,sd->thd", attn_weights, value_rows, preferred_element_type=jnp.float32
    )
    return attended.astype(jnp.bfloat16).reshape(token_count, -1)


def gather_features(rows_local):
    return lax.all_gather(rows_local, ("sec", "mp"), axis=1, tiled=True)


def section_features(rows_local, gain_row, allowed, positions, q_local, kv_local, o_local):
    share = rows_local.shape[1]
    square_sums = lax.psum(jnp.sum(rows_local * rows_local, axis=1), ("sec", "mp"))
    factor = lax.rsqrt(square_sums / D + rms_eps)
    gain_local = lax.dynamic_slice_in_dim(
        gain_row, lax.axis_index(("sec", "mp")) * share, share, 0
    ).astype(jnp.float32)
    normed_local = (rows_local * factor[:, None] * gain_local[None, :]).astype(jnp.bfloat16)
    normed = gather_features(normed_local)
    attended = attend(normed, allowed, positions, q_local, kv_local)
    summed = lax.psum_scatter(
        lax.dot_general(
            o_local, attended, (((0,), (1,)), ((), ())), preferred_element_type=jnp.float32
        ),
        ("sec", "mp"),
        scatter_dimension=0,
        tiled=True,
    )
    return rows_local + summed.T


def merger_front(patch_rows, ln_gain, ln_shift, w_in_full, b_in, w_out_full, b_out):
    normed = group_norm(patch_rows, ln_gain, ln_shift).astype(jnp.bfloat16)
    pre_act = jnp.dot(normed, w_in_full, preferred_element_type=jnp.float32) + b_in.astype(
        jnp.float32
    )
    hidden_units = gelu_exact(pre_act).astype(jnp.bfloat16)
    partial_out = jnp.dot(hidden_units, w_out_full, preferred_element_type=jnp.float32)
    merged = lax.psum_scatter(
        partial_out, ("sec", "mp"), scatter_dimension=1, tiled=True
    ) + b_out.astype(jnp.float32)
    return (merged.astype(jnp.bfloat16), pre_act)


def merger_back(patch_rows, pre_act, hidden_grads, ln_gain, ln_shift, w_in_full):
    _, pull_gelu = jax.vjp(gelu_exact, pre_act)
    pre_grads = pull_gelu(hidden_grads)[0].astype(jnp.bfloat16)
    normed_grads = lax.dot_general(
        pre_grads, w_in_full, (((1,), (1,)), ((), ())), preferred_element_type=jnp.float32
    )
    normed_grads = lax.psum(normed_grads, ("sec", "mp"))
    _, pull_norm = jax.vjp(
        lambda values: group_norm(values, ln_gain, ln_shift), patch_rows.astype(jnp.float32)
    )
    return pull_norm(normed_grads)[0]


def local(
    patches,
    ln_gain,
    ln_shift,
    w_in,
    b_in,
    w_out,
    b_out,
    place,
    image_counts,
    text_rows,
    segments,
    norm_gain,
    q_weight,
    kv_weight,
    o_weight,
    grad_rows,
):
    w_in_full, w_out_full = (
        lax.all_gather(w_in, "dp", axis=0, tiled=True),
        lax.all_gather(w_out, "dp", axis=1, tiled=True),
    )
    slot_count = patches.shape[0]
    tokens = text_rows.shape[0]
    slot_index = jnp.arange(slot_count, dtype=jnp.int32)
    live_slot = slot_index < image_counts[0]
    slot_grads = jnp.where(live_slot[:, None], grad_rows, jnp.zeros_like(grad_rows))
    hidden_grads = lax.dot_general(
        slot_grads, w_out_full, (((1,), (1,)), ((), ())), preferred_element_type=jnp.float32
    )
    merged_local, pre_act = merger_front(
        patches, ln_gain, ln_shift, w_in_full, b_in, w_out_full, b_out
    )
    patch_grads = merger_back(patches, pre_act, hidden_grads, ln_gain, ln_shift, w_in_full)
    token_index = jnp.arange(tokens, dtype=jnp.int32)
    select = (place[:, None] == token_index[None, :]) & live_slot[:, None]
    is_image = jnp.any(select, axis=0)
    picked = lax.dot_general(
        select.astype(jnp.bfloat16),
        merged_local,
        (((0,), (0,)), ((), ())),
        preferred_element_type=jnp.float32,
    )
    start_rows = jnp.where(is_image[:, None], picked, text_rows.astype(jnp.float32)).astype(
        jnp.bfloat16
    )
    allowed, positions = doc_mask(segments[0])
    layer_count = q_weight.shape[0]
    current = start_rows.astype(jnp.float32)
    for layer_index in range(layer_count):
        current = section_features(
            current,
            norm_gain[layer_index],
            allowed,
            positions,
            q_weight[layer_index],
            kv_weight[layer_index],
            o_weight[layer_index],
        )
    return (current, patch_grads)


def solution(mesh):
    in_specs = (
        P("dp", None),
        P(),
        P(),
        P("dp", ("sec", "mp")),
        P(("sec", "mp")),
        P(("sec", "mp"), "dp"),
        P(("sec", "mp")),
        P("dp"),
        P("dp"),
        P("dp", ("sec", "mp")),
        P("dp", None),
        P(),
        P(None, None, ("sec", "mp")),
        P(None, None, ("sec", "mp"), None),
        P(None, ("sec", "mp"), None),
        P("dp", None),
    )
    out_specs = (P("dp", ("sec", "mp")), P("dp", None))
    return jax.shard_map(local, mesh=mesh, in_specs=in_specs, out_specs=out_specs, check_vma=False)
```

profile of v0, /device:TPU:0, one launch (start us, length us, event | category | flops | bytes accessed | tf_op | source)
XLA Modules:
  0.0 707.5 jit_solution(7781813747117255810)
XLA Ops:
  7.2 0.7 all-gather.5.cloned.1.call-update
  8.0 0.7 all-gather.7.cloned.1.call-update
  8.7 1.4 reshape.223
  10.4 0.4 multiply_reduce_fusion.1
  11.5 64.8 %all-gather.5.cloned.1.call-done = bf16[5120,320]{0,1:T(8,128)(2,1)} async-done(((bf16[640,320]{0,1:T(8,128)(2,1)}), bf16[5120,320]{0,1:T(8,128)(2,1)}) %all-gather.5.cloned.1.call-update) | async-done | bytes 3276816 | tf_op jit(solution)/shard_map/all_gather | solution.py:145
  76.3 3.0 convolution_add_fusion
  79.4 77.0 %all-gather.7.cloned.1.call-done = bf16[320,8192]{1,0:T(8,128)(2,1)} async-done(((bf16[320,1024]{1,0:T(8,128)(2,1)}), bf16[320,8192]{1,0:T(8,128)(2,1)}) %all-gather.7.cloned.1.call-update) | async-done | bytes 5242896 | tf_op jit(solution)/shard_map/all_gather | solution.py:146
  156.4 4.6 fusion.88
  162.0 60.0 %reduce-scatter.4.cloned.1.call-done = f32[40,512]{1,0:T(8,128)} async-done(((f32[40,8192]{1,0:T(8,128)}), f32[40,512]{1,0:T(8,128)}) %reduce-scatter.4.cloned.1.call-update) | async-done | bytes 81936 | tf_op jit(solution)/shard_map/reduce_scatter | solution.py:107
  222.0 1.4 multiply_reduce_fusion.3
  223.4 27.7 %psum.21 = f32[256]{0:T(256)S(1)} all-reduce(f32[256]{0:T(256)S(1)} %get-tuple-element.16), channel_id=1, replica_groups=mesh['sec'=4,'dp'=8,'mp'=4] {'sec','mp'}, use_global_device_ids=true, to_apply=%region_5.6 | all-reduce | flops 256 | bytes 2048 | tf_op jit(solution)/shard_map/psum | solution.py:81
  251.1 0.8 multiply_convert_fusion.1
  252.0 5.7 slice_bitcast_fusion.1
  257.8 6.4 copy.26
  264.5 0.3 multiply_cosine_fusion
  264.8 23.3 %all-gather.9.cloned.1.call-done = bf16[256,8192]{1,0:T(8,128)(2,1)} async-done(((bf16[256,512]{1,0:T(8,128)(2,1)}), bf16[256,8192]{1,0:T(8,128)(2,1)}) %all-gather.9.cloned.1.call-update) | async-done | bytes 4194320 | tf_op jit(solution)/shard_map/all_gather | solution.py:76
  288.1 4.0 fusion.10
  292.1 5.8 all_gather.21
  297.9 0.3 fusion.52
  298.3 3.5 fusion.8
  301.8 0.6 copy-done.12
  302.4 1.0 fusion.21
  303.5 1.2 fusion.117
  304.7 1.6 convolution_convert_fusion.1
  306.3 6.7 convolution_bitcast_fusion.1
  313.1 97.8 %reduce-scatter.6.cloned.1.call-done = f32[512,256]{0,1:T(8,128)} async-done(((f32[8192,256]{0,1:T(8,128)}), f32[512,256]{0,1:T(8,128)}) %reduce-scatter.6.cloned.1.call-update) | async-done | bytes 524304 | tf_op jit(solution)/shard_map/reduce_scatter | solution.py:89
  410.9 1.2 multiply_reduce_fusion.2
  412.1 27.6 %psum.22 = f32[256]{0:T(256)S(1)} all-reduce(f32[256]{0:T(256)S(1)} %multiply_reduce_fusion.2), channel_id=1, replica_groups=mesh['sec'=4,'dp'=8,'mp'=4] {'sec','mp'}, use_global_device_ids=true, to_apply=%region_11.12 | all-reduce | flops 256 | bytes 2048 | tf_op jit(solution)/shard_map/psum | solution.py:81
  439.7 1.9 multiply_convert_fusion
  441.8 6.5 copy.30
  448.3 7.6 %fusion.71 = f32[40,5120]{1,0:T(8,128)} fusion(bf16[5120,320]{0,1:T(8,128)(2,1)} %all-gather.5.cloned.1.call-done, bf16[320,8192]{1,0:T(8,128)(2,1)} %all-gather.7.cloned.1.call-done, bf16[40,8192]{1,0:T(8,128)(2,1)S(1)} %copy-done.7, pred[40]{0:T(512)(128)(4,1)S(1)} %iota_compare_fusion.2, f32[40,320]{1,0:T(8,128)S(1)} %convolution_add_fusion), kind=kOutput, calls=%fused_computation.107 | convolution fusion | flops 342036480 | bytes 10045480 | tf_op jit(solution)/shard_map/dot_general | solution.py:116
  456.0 21.5 %all-gather.11.cloned.1.call-done = bf16[256,8192]{1,0:T(8,128)(2,1)} async-done(((bf16[256,512]{1,0:T(8,128)(2,1)}), bf16[256,8192]{1,0:T(8,128)(2,1)}) %all-gather.11.cloned.1.call-update) | async-done | bytes 4194320 | tf_op jit(solution)/shard_map/all_gather | solution.py:76
  477.5 4.0 fusion.5
  481.5 5.8 all_gather.23
  487.3 0.3 fusion.56
  487.6 3.5 fusion.3
  491.2 0.6 copy-done.11
  491.8 1.0 fusion.19
  492.9 1.2 fusion.120
  494.1 1.6 convolution_convert_fusion
  495.7 6.7 convolution_bitcast_fusion
  502.4 97.3 %all-reduce.2.cloned.1.call-done = f32[40,5120]{1,0:T(8,128)} async-done(((f32[40,5120]{1,0:T(8,128)}), f32[40,5120]{1,0:T(8,128)}) %all-reduce.2.cloned.1.call-update) | async-done | bytes 819216 | tf_op jit(solution)/shard_map/psum | solution.py:119
  599.7 1.5 reshape.226
  601.3 0.4 multiply_reduce_fusion
  601.7 0.6 fusion.29
  603.0 1.2 fusion.28
  604.2 94.5 %reduce-scatter.8.cloned.1.call-done = f32[512,256]{0,1:T(8,128)} async-done(((f32[8192,256]{0,1:T(8,128)}), f32[512,256]{0,1:T(8,128)}) %reduce-scatter.8.cloned.1.call-update) | async-done | bytes 524304 | tf_op jit(solution)/shard_map/reduce_scatter | solution.py:89
  698.7 2.0 bitcast_add_fusion
  (87 shorter events, 2.8 us)
Async XLA Ops:
  7.2 69.2 %all-gather.5.cloned.1.call-start = ((), (), s32[]{:S(2)}) async-start(), calls=%async_computation.3 | async-start | bytes 3686400 | tf_op jit(solution)/shard_map/all_gather | solution.py:145
  7.9 3.5 copy-start.16
  7.9 3.6 copy-start.17
  7.9 148.5 %all-gather.7.cloned.1.call-start = ((), (), s32[]{:S(2)}) async-start(), calls=%async_computation.4 | async-start | bytes 5898240 | tf_op jit(solution)/shard_map/all_gather | solution.py:146
  8.7 2.8 copy-start.18
  8.7 67.7 %copy-start.5 = (bf16[40,5120]{1,0:T(8,128)(2,1)S(1)}, bf16[40,5120]{1,0:T(8,128)(2,1)}, u32[]{:S(2)}) copy-start(bf16[40,5120]{1,0:T(8,128)(2,1)} %param.16) | copy-start | bytes 1228804
  8.7 213.3 %reduce-scatter.4.cloned.1.call-start = ((), (), s32[]{:S(2)}) async-start(), calls=%async_computation.5 | async-start | bytes 1392640 | tf_op jit(solution)/shard_map/reduce_scatter | solution.py:107
  11.4 149.7 %copy-start = (f32[5,8,4,1280]{3,1,2,0:T(8,128)}, f32[5,8,4,1280]{3,1,2,0:T(8,128)S(1)}, u32[]{:S(2)}) copy-start(f32[5,8,4,1280]{3,1,2,0:T(8,128)S(1)} %copy.42) | copy-start | bytes 2457604
  79.4 82.4 %copy-start.19 = (bf16[512]{0:T(512)(128)(2,1)S(1)}, bf16[512]{0:T(512)(128)(2,1)}, u32[]{:S(2)}) copy-start(bf16[512]{0:T(512)(128)(2,1)} %param.22) | copy-start | bytes 3076
  79.4 82.5 %copy-start.8 = (bf16[2,8192]{1,0:T(2,128)(2,1)S(1)}, bf16[2,8192]{1,0:T(2,128)(2,1)}, u32[]{:S(2)}) copy-start(bf16[2,8192]{1,0:T(2,128)(2,1)} %param.27) | copy-start | bytes 98308
  79.4 82.5 %copy-start.20 = (s32[40]{0:T(128)S(1)}, s32[40]{0:T(128)}, u32[]{:S(2)}) copy-start(s32[40]{0:T(128)} %param.23) | copy-start | bytes 484
  161.1 127.0 %all-gather.9.cloned.1.call-start = ((), (), s32[]{:S(2)}) async-start(), calls=%async_computation.6 | async-start | bytes 4456448 | tf_op jit(solution)/shard_map/all_gather | solution.py:76
  252.0 158.9 %reduce-scatter.6.cloned.1.call-start = ((), (), s32[]{:S(2)}) async-start(), calls=%async_computation.7 | async-start | bytes 8912896 | tf_op jit(solution)/shard_map/reduce_scatter | solution.py:89
  257.8 6.4 copy-start.15
  264.4 39.0 %copy-start.9 = (pred[256,256]{0,1:T(8,128)(4,1)}, pred[256,256]{0,1:T(8,128)(4,1)S(1)}, u32[]{:S(2)}) copy-start(pred[256,256]{0,1:T(8,128)(4,1)S(1)} %fusion.36) | copy-start | bytes 196612
  288.1 10.2 %copy-start.4 = (bf16[256,8192]{1,0:T(8,128)(2,1)S(1)}, bf16[256,8192]{1,0:T(8,128)(2,1)}, u32[]{:S(2)}) copy-start(bf16[256,8192]{1,0:T(8,128)(2,1)} %copy.26) | copy-start | bytes 12582916
  298.2 3.6 copy-start.13
  298.2 3.6 copy-start.14
  301.8 0.6 copy-start.12
  313.0 164.4 %all-gather.11.cloned.1.call-start = ((), (), s32[]{:S(2)}) async-start(), calls=%async_computation.8 | async-start | bytes 4456448 | tf_op jit(solution)/shard_map/all_gather | solution.py:76
  441.6 158.2 %all-reduce.2.cloned.1.call-start = ((), (), s32[]{:S(2)}) async-start(), calls=%async_computation.10 | async-start | bytes 1638400 | tf_op jit(solution)/shard_map/psum | solution.py:119
  441.8 6.5 copy-start.7
  455.9 242.8 %reduce-scatter.8.cloned.1.call-start = ((), (), s32[]{:S(2)}) async-start(), calls=%async_computation.9 | async-start | bytes 8912896 | tf_op jit(solution)/shard_map/reduce_scatter | solution.py:89
  477.5 10.1 %copy-start.3 = (bf16[256,8192]{1,0:T(8,128)(2,1)S(1)}, bf16[256,8192]{1,0:T(8,128)(2,1)}, u32[]{:S(2)}) copy-start(bf16[256,8192]{1,0:T(8,128)(2,1)} %copy.30) | copy-start | bytes 12582916
  487.6 4.2 copy-start.10
  491.2 0.6 copy-start.11
  601.3 1.7 copy-start.1
  601.3 1.7 copy-start.6
  602.6 96.1 %copy-start.2 = (f32[512,256]{0,1:T(8,128)S(1)}, f32[512,256]{0,1:T(8,128)}, u32[]{:S(2)}) copy-start(f32[512,256]{0,1:T(8,128)} %reduce-scatter.6.cloned.1.call-done) | copy-start | bytes 1572868
Sparse Core Ops, SparseCore 0:
  10.4 65.9 all-gather.4
  78.6 77.7 all-gather.6
  161.2 60.7 reduce-scatter.3
  252.1 35.9 all-gather.8
  313.2 97.6 reduce-scatter.5
  441.7 35.7 all-gather.10
  480.5 119.1 all-reduce.1
  602.1 96.5 reduce-scatter.7
where the time goes:
time: 709 us; the launch traced here: 708 us
  waiting for transfers between devices  538 us (76%)
  blocking collectives  66.9 us (9%)
  matrix products  52.9 us (7%)
  local copies, waits for them, and re-layouts  24.3 us (3%)
  between operations  15.3 us (2%)
  other arithmetic  9.97 us (1%)
    reduce_scatter x2, waiting for transfers between devices, section_features(): lax.psum_scatter(lax.dot_general(o_local, attended, (((0,), (1,)), ((), (...  192 us
    psum x1, waiting for transfers between devices, merger_back(): normed_grads = lax.psum(normed_grads, ('sec', 'mp'))  97.3 us
    all_gather x1, waiting for transfers between devices, local(): lax.all_gather(w_out, 'dp', axis=1, tiled=True)  77 us
    all_gather x1, waiting for transfers between devices, local(): lax.all_gather(w_in, 'dp', axis=0, tiled=True)  64.8 us
    reduce_scatter x1, waiting for transfers between devices, merger_front(): lax.psum_scatter(partial_out, ('sec', 'mp'), scatter_dimension=1, tiled=T...  60 us
    psum x2, blocking collectives, section_features(): lax.psum(jnp.sum(rows_local * rows_local, axis=1), ('sec', 'mp'))  55.3 us
    all_gather x2, waiting for transfers between devices, gather_features(): return lax.all_gather(rows_local, ('sec', 'mp'), axis=1, tiled=True)  44.8 us
    dot_general x3, local copies, waits for them, and re-layouts, attend(): jnp.dot(normed, q_local, preferred_element_type=jnp.float32)  18.6 us
  transfers between devices with their start and end apart: 8, of which 8 were waited for; matrix products, arithmetic and copies ran while one was open for 8% of the time, Pallas kernels for 0%

commit v1 on v0

--- a/solution.py
+++ b/solution.py
@@ -143,7 +143,9 @@
 ):
     w_in_full, w_out_full = (
         lax.all_gather(w_in, "dp", axis=0, tiled=True),
-        lax.all_gather(w_out, "dp", axis=1, tiled=True),
+        jnp.concatenate(
+            lax.all_to_all(jnp.stack([w_out] * lax.axis_size("dp")), "dp", 0, 0), axis=1
+        ),
     )
     slot_count = patches.shape[0]
     tokens = text_rows.shape[0]

time: 709 us -> 679 us (0.958)
  waiting for transfers between devices: 538 us -> 493 us
  local copies, waits for them, and re-layouts: 24.3 us -> 33.3 us
  starting transfers between devices: 0.5 us -> 8.49 us
    all_gather x1 -> x0, waiting for transfers between devices: 77 us -> none  [local(): lax.all_gather(w_out, 'dp', axis=1, tiled=True)]
    all_to_all x0 -> x1, waiting for transfers between devices: none -> 64.6 us  [local(): lax.all_to_all(jnp.stack([w_out] * lax.axis_size('dp')), 'dp', 0, 0)]
    all_gather x1, waiting for transfers between devices: 64.8 us -> 34.2 us  [local(): lax.all_gather(w_in, 'dp', axis=0, tiled=True)]
    all_to_all x0 -> x1, starting transfers between devices: none -> 8.02 us  [local(): lax.all_to_all(jnp.stack([w_out] * lax.axis_size('dp')), 'dp', 0, 0)]
  transfers between devices with their start and end apart: 8 -> 8, of which waited for: 8 -> 8; matrix products, arithmetic and copies ran while one was open for 8% -> 9% of each run, Pallas kernels for 0% -> 0%
where the time goes in v1:
time: 679 us; the launch traced here: 678 us
  waiting for transfers between devices  493 us (73%)
  blocking collectives  66.8 us (10%)
  matrix products  50.5 us (7%)
  local copies, waits for them, and re-layouts  33.3 us (5%)
  between operations  15.2 us (2%)
  other arithmetic  10.6 us (2%)
  starting transfers between devices  8.49 us (1%)
    reduce_scatter x2, waiting for transfers between devices, section_features(): lax.psum_scatter(lax.dot_general(o_local, attended, (((0,), (1,)), ((), (...  192 us
    psum x1, waiting for transfers between devices, merger_back(): normed_grads = lax.psum(normed_grads, ('sec', 'mp'))  98 us
    all_to_all x1, waiting for transfers between devices, local(): lax.all_to_all(jnp.stack([w_out] * lax.axis_size('dp')), 'dp', 0, 0)  64.6 us
    reduce_scatter x1, waiting for transfers between devices, merger_front(): lax.psum_scatter(partial_out, ('sec', 'mp'), scatter_dimension=1, tiled=T...  59.3 us
    psum x2, blocking collectives, section_features(): lax.psum(jnp.sum(rows_local * rows_local, axis=1), ('sec', 'mp'))  55.3 us
    all_gather x2, waiting for transfers between devices, gather_features(): return lax.all_gather(rows_local, ('sec', 'mp'), axis=1, tiled=True)  44.8 us
    all_gather x1, waiting for transfers between devices, local(): lax.all_gather(w_in, 'dp', axis=0, tiled=True)  34.2 us
    dot_general x3, local copies, waits for them, and re-layouts, attend(): jnp.dot(normed, q_local, preferred_element_type=jnp.float32)  18.5 us
  transfers between devices with their start and end apart: 8, of which 8 were waited for; matrix products, arithmetic and copies ran while one was open for 9% of the time, Pallas kernels for 0%

profile of v1, /device:TPU:0, one launch (start us, length us, event | category | flops | bytes accessed | tf_op | source)
XLA Modules:
  0.0 678.3 jit_solution(6715559119171740778)
XLA Ops:
  7.2 0.7 all-gather.4.cloned.1.call-update
  7.9 4.1 stack.2
  12.0 8.0 %all-to-all-start = ((bf16[8,320,1024]{2,1,0:T(8,128)(2,1)}), bf16[8,320,1024]{2,1,0:T(8,128)(2,1)}, u32[]{:S(2)}, u32[]{:S(2)}) async-start(bf16[8,320,1024]{2,1,0:T(8,128)(2,1)} %stack.2), calls=%async_computation | async-start | bytes 10485760 | tf_op jit(solution)/shard_map/all_to_all | solution.py:147
  20.1 0.4 reshape.231
  20.7 0.4 multiply_reduce_fusion.1
  21.9 64.6 %all-to-all-done = bf16[8,320,1024]{2,1,0:T(8,128)(2,1)} async-done(((bf16[8,320,1024]{2,1,0:T(8,128)(2,1)}), bf16[8,320,1024]{2,1,0:T(8,128)(2,1)}, u32[]{:S(2)}, u32[]{:S(2)}) %all-to-all-start) | async-done | bytes 5242912 | tf_op jit(solution)/shard_map/all_to_all | solution.py:147
  86.5 5.7 copy.60
  92.2 34.2 %all-gather.4.cloned.1.call-done = bf16[5120,320]{0,1:T(8,128)(2,1)} async-done(((bf16[640,320]{0,1:T(8,128)(2,1)}), bf16[5120,320]{0,1:T(8,128)(2,1)}) %all-gather.4.cloned.1.call-update) | async-done | bytes 3276816 | tf_op jit(solution)/shard_map/all_gather | solution.py:145
  126.4 3.2 convolution_add_fusion
  129.9 2.2 fusion.88
  132.8 0.7 fusion.116
  133.6 59.3 %reduce-scatter.4.cloned.1.call-done = f32[40,512]{1,0:T(8,128)} async-done(((f32[40,8192]{1,0:T(8,128)}), f32[40,512]{1,0:T(8,128)}) %reduce-scatter.4.cloned.1.call-update) | async-done | bytes 81936 | tf_op jit(solution)/shard_map/reduce_scatter | solution.py:107
  192.9 1.3 multiply_reduce_fusion.3
  194.2 27.7 %psum.21 = f32[256]{0:T(256)S(1)} all-reduce(f32[256]{0:T(256)S(1)} %get-tuple-element.16), channel_id=1, replica_groups=mesh['sec'=4,'dp'=8,'mp'=4] {'sec','mp'}, use_global_device_ids=true, to_apply=%region_5.6 | all-reduce | flops 256 | bytes 2048 | tf_op jit(solution)/shard_map/psum | solution.py:81
  221.9 0.8 multiply_convert_fusion.1
  222.8 5.7 slice_bitcast_fusion.1
  228.5 6.4 copy.44
  235.5 23.4 %all-gather.6.cloned.1.call-done = bf16[256,8192]{1,0:T(8,128)(2,1)} async-done(((bf16[256,512]{1,0:T(8,128)(2,1)}), bf16[256,8192]{1,0:T(8,128)(2,1)}) %all-gather.6.cloned.1.call-update) | async-done | bytes 4194320 | tf_op jit(solution)/shard_map/all_gather | solution.py:76
  258.9 4.0 fusion.10
  262.9 5.8 all_gather.17
  269.0 3.5 fusion.8
  272.6 0.6 copy-done.10
  273.2 1.1 fusion.21
  274.2 1.2 fusion.117
  275.5 1.6 convolution_convert_fusion.1
  277.1 6.7 convolution_bitcast_fusion.1
  283.8 0.7 dynamic-slice_convert_fusion
  284.5 97.1 %reduce-scatter.6.cloned.1.call-done = f32[512,256]{0,1:T(8,128)} async-done(((f32[8192,256]{0,1:T(8,128)}), f32[512,256]{0,1:T(8,128)}) %reduce-scatter.6.cloned.1.call-update) | async-done | bytes 524304 | tf_op jit(solution)/shard_map/reduce_scatter | solution.py:89
  381.6 1.2 multiply_reduce_fusion.2
  382.8 27.6 %psum.22 = f32[256]{0:T(256)S(1)} all-reduce(f32[256]{0:T(256)S(1)} %multiply_reduce_fusion.2), channel_id=1, replica_groups=mesh['sec'=4,'dp'=8,'mp'=4] {'sec','mp'}, use_global_device_ids=true, to_apply=%region_11.12 | all-reduce | flops 256 | bytes 2048 | tf_op jit(solution)/shard_map/psum | solution.py:81
  410.4 1.9 multiply_convert_fusion
  412.5 6.4 copy.48
  418.9 7.8 %fusion.71 = f32[40,5120]{1,0:T(8,128)} fusion(bf16[5120,320]{0,1:T(8,128)(2,1)} %all-gather.4.cloned.1.call-done, bf16[320,8192]{1,0:T(8,128)(2,1)} %bitcast.120, bf16[40,8192]{1,0:T(8,128)(2,1)} %param.31, pred[40]{0:T(512)(128)(4,1)S(1)} %iota_compare_fusion.2, f32[40,320]{1,0:T(8,128)S(1)} %convolution_add_fusion), kind=kOutput, calls=%fused_computation.107 | convolution fusion | flops 342036480 | bytes 10045480 | tf_op jit(solution)/shard_map/dot_general | solution.py:116
  426.8 21.4 %all-gather.8.cloned.1.call-done = bf16[256,8192]{1,0:T(8,128)(2,1)} async-done(((bf16[256,512]{1,0:T(8,128)(2,1)}), bf16[256,8192]{1,0:T(8,128)(2,1)}) %all-gather.8.cloned.1.call-update) | async-done | bytes 4194320 | tf_op jit(solution)/shard_map/all_gather | solution.py:76
  448.2 4.0 fusion.5
  452.2 5.8 all_gather.19
  458.4 3.5 fusion.3
  461.9 1.0 fusion.19
  463.0 1.1 fusion.120
  464.1 1.6 convolution_convert_fusion
  465.7 6.7 convolution_bitcast_fusion
  472.5 98.0 %all-reduce.2.cloned.1.call-done = f32[40,5120]{1,0:T(8,128)} async-done(((f32[40,5120]{1,0:T(8,128)}), f32[40,5120]{1,0:T(8,128)}) %all-reduce.2.cloned.1.call-update) | async-done | bytes 819216 | tf_op jit(solution)/shard_map/psum | solution.py:119
  570.5 1.5 reshape.236
  572.1 0.4 multiply_reduce_fusion
  572.5 0.6 fusion.29
  573.8 1.2 fusion.28
  574.9 94.5 %reduce-scatter.8.cloned.1.call-done = f32[512,256]{0,1:T(8,128)} async-done(((f32[8192,256]{0,1:T(8,128)}), f32[512,256]{0,1:T(8,128)}) %reduce-scatter.8.cloned.1.call-update) | async-done | bytes 524304 | tf_op jit(solution)/shard_map/reduce_scatter | solution.py:89
  669.5 2.0 bitcast_add_fusion
  (86 shorter events, 3.9 us)
Async XLA Ops:
  7.2 119.2 %all-gather.4.cloned.1.call-start = ((), (), s32[]{:S(2)}) async-start(), calls=%async_computation.4 | async-start | bytes 3686400 | tf_op jit(solution)/shard_map/all_gather | solution.py:145
  12.0 8.1 %copy-start.6 = (bf16[40,5120]{1,0:T(8,128)(2,1)S(1)}, bf16[40,5120]{1,0:T(8,128)(2,1)}, u32[]{:S(2)}) copy-start(bf16[40,5120]{1,0:T(8,128)(2,1)} %param.16) | copy-start | bytes 1228804
  12.0 74.4 %all-to-all-start = ((bf16[8,320,1024]{2,1,0:T(8,128)(2,1)}), bf16[8,320,1024]{2,1,0:T(8,128)(2,1)}, u32[]{:S(2)}, u32[]{:S(2)}) async-start(bf16[8,320,1024]{2,1,0:T(8,128)(2,1)} %stack.2), calls=%async_computation | async-start | bytes 10485760 | tf_op jit(solution)/shard_map/all_to_all | solution.py:147
  20.0 1.7 copy-start.15
  20.0 1.8 copy-start.16
  20.0 1.8 copy-start.17
  20.1 172.8 %reduce-scatter.4.cloned.1.call-start = ((), (), s32[]{:S(2)}) async-start(), calls=%async_computation.5 | async-start | bytes 1392640 | tf_op jit(solution)/shard_map/reduce_scatter | solution.py:107
  21.8 104.6 %copy-start.1 = (f32[5,8,4,1280]{3,1,2,0:T(8,128)}, f32[5,8,4,1280]{3,1,2,0:T(8,128)S(1)}, u32[]{:S(2)}) copy-start(f32[5,8,4,1280]{3,1,2,0:T(8,128)S(1)} %copy.61) | copy-start | bytes 2457604
  126.4 3.5 copy-start
  129.9 2.9 copy-start.18
  129.9 2.9 copy-start.9
  129.9 3.6 copy-start.19
  129.9 63.0 %copy-start.8 = (bf16[256,512]{1,0:T(8,128)(2,1)S(1)}, bf16[256,512]{1,0:T(8,128)(2,1)}, u32[]{:S(2)}) copy-start(bf16[256,512]{1,0:T(8,128)(2,1)} %param.25) | copy-start | bytes 786436
  132.0 126.8 %all-gather.6.cloned.1.call-start = ((), (), s32[]{:S(2)}) async-start(), calls=%async_computation.6 | async-start | bytes 4456448 | tf_op jit(solution)/shard_map/all_gather | solution.py:76
  222.8 158.9 %reduce-scatter.6.cloned.1.call-start = ((), (), s32[]{:S(2)}) async-start(), calls=%async_computation.7 | async-start | bytes 8912896 | tf_op jit(solution)/shard_map/reduce_scatter | solution.py:89
  228.5 6.5 copy-start.14
  258.9 10.1 %copy-start.5 = (bf16[256,8192]{1,0:T(8,128)(2,1)S(1)}, bf16[256,8192]{1,0:T(8,128)(2,1)}, u32[]{:S(2)}) copy-start(bf16[256,8192]{1,0:T(8,128)(2,1)} %copy.44) | copy-start | bytes 12582916
  269.0 3.6 copy-start.13
  272.6 0.6 copy-start.10
  283.8 164.4 %all-gather.8.cloned.1.call-start = ((), (), s32[]{:S(2)}) async-start(), calls=%async_computation.8 | async-start | bytes 4456448 | tf_op jit(solution)/shard_map/all_gather | solution.py:76
  412.3 158.2 %all-reduce.2.cloned.1.call-start = ((), (), s32[]{:S(2)}) async-start(), calls=%async_computation.10 | async-start | bytes 1638400 | tf_op jit(solution)/shard_map/psum | solution.py:119
  426.8 242.7 %reduce-scatter.8.cloned.1.call-start = ((), (), s32[]{:S(2)}) async-start(), calls=%async_computation.9 | async-start | bytes 8912896 | tf_op jit(solution)/shard_map/reduce_scatter | solution.py:89
  448.2 10.2 %copy-start.4 = (bf16[256,8192]{1,0:T(8,128)(2,1)S(1)}, bf16[256,8192]{1,0:T(8,128)(2,1)}, u32[]{:S(2)}) copy-start(bf16[256,8192]{1,0:T(8,128)(2,1)} %copy.48) | copy-start | bytes 12582916
  458.3 3.6 copy-start.11
  458.4 3.6 copy-start.12
  572.0 1.7 copy-start.2
  572.0 1.7 copy-start.7
  573.4 96.1 %copy-start.3 = (f32[512,256]{0,1:T(8,128)S(1)}, f32[512,256]{0,1:T(8,128)}, u32[]{:S(2)}) copy-start(f32[512,256]{0,1:T(8,128)} %reduce-scatter.6.cloned.1.call-done) | copy-start | bytes 1572868
Sparse Core Ops, SparseCore 0:
  10.4 115.9 all-gather.3
  132.2 60.6 reduce-scatter.3
  222.9 35.9 all-gather.5
  283.9 97.6 reduce-scatter.5
  412.4 35.7 all-gather.7
  451.1 119.3 all-reduce.1
  572.9 96.5 reduce-scatter.7
